TPU v7x, 32 devices: a whole 2x2x4 slice. The times are simulated.
32 devices in a mesh: group: 2 (over y), gene: 4 (over z), lat: 2 (over x), sub: 2 (over core).
Axes of the slice: x: 2, y: 2, z: 4, core: 2. Of those that a mesh axis runs over, the one named last changes fastest.
Arguments:
- cell_index: int32 [2048], P(('group', 'lat', 'sub')), parts along dimension 0, may hold values from 0 to 511
- coords_table: float32 [4, 2048], P('group', ('lat', 'sub')), parts along dimension 0, may hold values from 0 to 1
- expr_table: bfloat16 [4096, 16384], P(('group', 'lat', 'sub'), 'gene'), parts along dimension 0, may hold values from -6 to 6
- inducing: float32 [4, 64, 8192], P('group', 'lat', 'sub'), parts along dimension 0, may hold values from 0 to 1
- ind_weights: float32 [128, 8192], P(('group', 'lat'), 'sub'), parts along dimension 0, may hold values from -0.6 to 0.6
- lengthscale: float32 [128], P(('group', 'lat')), parts along dimension 0, may hold values from 0.02 to 0.1
- variance: float32 [128], P(('group', 'lat')), parts along dimension 0, may hold values from 0.5 to 2
- mixing: bfloat16 [128, 16384], P('group', 'gene'), parts along dimension 0, may hold values from -0.75 to 0.75
- noise_prec: float32 [32768], P(('group', 'gene')), parts along dimension 0, may hold values from 0.5 to 4
Outputs:
- grad_mixing: float32 [128, 16384], P('group', 'gene'), parts along dimension 0
- grad_inducing: float32 [128, 8192], P(('group', 'lat'), 'sub'), parts along dimension 0
There are 2 independent parts, one for each index of `group`. A program takes and returns all parts, laid end to end along the dimension named above; each array names one. Nothing has to cross between parts.
Inputs may be any that keep to these rules, and one draw needn't show every extreme that they name: Entry n indexes a row inside block n // 256 of the tables: cell n is table row (n // 256) * 512 + cell_index[n]; cells may repeat.
All inputs are finite; a program needn't handle non-finite values.
Results may differ from a plain program's by a relative error of at most 0.00075.
Values may be sent and summed in bfloat16 or wider, within the bound.
A program may use at most 64 MiB of HBM per device.

v0:
```python
import math

import jax
import jax.numpy as jnp
from jax import lax
from jax.sharding import PartitionSpec as P


def kernel_tile(cell_xy, points, length, height):
    delta_x = cell_xy[0][:, None] - points[0][None, :]
    delta_y = cell_xy[1][:, None] - points[1][None, :]
    return height * jnp.exp(-(delta_x * delta_x + delta_y * delta_y) * (0.5 / (length * length)))


def on_device(
    cell_index,
    coords_table,
    expr_table,
    inducing,
    ind_weights,
    lengthscale,
    variance,
    mixing,
    noise_prec,
):
    gene_count = lax.axis_size("gene")
    lat_count = lax.axis_size("lat")
    sub_count = lax.axis_size("sub")
    bat_rows = cell_index.shape[0]
    per_block = bat_rows // gene_count
    block_count = lat_count * sub_count
    gene_place = lax.axis_index("gene")
    local_xy = jnp.take(coords_table, cell_index, axis=1)
    every_xy = lax.all_gather(local_xy, ("lat", "sub"), axis=1, tiled=True)
    every_xy = every_xy.reshape(2, block_count, gene_count, per_block)
    kernel_xy = lax.dynamic_slice_in_dim(every_xy, gene_place, 1, 2).reshape(
        2, block_count * per_block
    )
    moved = jnp.moveaxis(inducing, 1, 0)

    def forward(packed):
        points, weights, length, height = packed
        return jnp.dot(
            kernel_tile(kernel_xy, points, length, height), weights, precision=lax.Precision.HIGHEST
        )

    local_latent = lax.map(forward, (moved, ind_weights, lengthscale, variance))
    swapped = lax.all_to_all(local_latent, "lat", split_axis=1, concat_axis=0, tiled=True)
    summed = lax.psum_scatter(swapped, "sub", scatter_dimension=1, tiled=True).astype(jnp.bfloat16)
    latent = lax.all_gather(summed, "gene", axis=1, tiled=True)
    observed = jnp.take(expr_table, cell_index, axis=0)
    predicted = lax.dot_general(
        latent, mixing, (((0,), (0,)), ((), ())), preferred_element_type=jnp.float32
    )
    weighted = (noise_prec[None, :] * (observed.astype(jnp.float32) - predicted)).astype(
        jnp.bfloat16
    )
    grad_scale = -1.0 / math.sqrt(bat_rows * block_count)
    mixing_term = grad_scale * jnp.dot(latent, weighted, preferred_element_type=jnp.float32)
    grad_mixing = lax.psum(mixing_term, ("lat", "sub"))
    cell_term = grad_scale * lax.dot_general(
        mixing, weighted, (((1,), (1,)), ((), ())), preferred_element_type=jnp.float32
    )
    shared = lax.psum_scatter(cell_term, "gene", scatter_dimension=1, tiled=True)
    paired = lax.all_gather(shared, "sub", axis=1, tiled=True)
    latent_grad = lax.all_to_all(paired, "lat", split_axis=0, concat_axis=1, tiled=True)

    def backward(packed):
        points, gradient, length, height = packed
        return jnp.dot(
            gradient,
            kernel_tile(kernel_xy, points, length, height),
            precision=lax.Precision.HIGHEST,
        )

    partial_inducing = lax.map(backward, (moved, latent_grad, lengthscale, variance))
    grad_inducing = lax.psum(partial_inducing, "gene")
    return (grad_mixing, grad_inducing)


def solution(mesh):
    in_specs = (
        P(("group", "lat", "sub")),
        P("group", ("lat", "sub")),
        P(("group", "lat", "sub"), "gene"),
        P("group", "lat", "sub"),
        P(("group", "lat"), "sub"),
        P(("group", "lat")),
        P(("group", "lat")),
        P("group", "gene"),
        P(("group", "gene")),
    )
    out_specs = (P("group", "gene"), P(("group", "lat"), "sub"))
    return jax.shard_map(
        on_device, mesh=mesh, in_specs=in_specs, out_specs=out_specs, check_vma=False
    )
```

profile of v0, /device:TPU:0, one launch (start us, length us, event | category | flops | bytes accessed | tf_op | source)
XLA Modules:
  0.0 743.6 jit_solution(11795437279426381336)
XLA Ops:
  10.3 8.6 %all_gather.9 = f32[2,1024]{0,1:T(8,128)S(1)} all-gather(f32[2,256]{0,1:T(8,128)S(1)} %select_bitcast_fusion), channel_id=1, replica_groups=mesh['group'=2,'gene'=4,'lat'=2,'sub'=2] {'lat','sub'}, dimensions={1}, use_global_device_ids=true | all-gather | bytes 10240 | tf_op jit(solution)/shard_map/all_gather | solution.py:34
  21.1 317.4 %while.20 = (s32[]{:T(128)}, f32[32,256]{1,0:T(8,128)S(1)}, f32[32]{0:T(128)}, f32[2,256]{1,0:T(2,128)S(1)}, f32[32,2,4096]{2,1,0:T(2,128)S(1)}, /*index=5*/f32[...) while((s32[]{:T(128)}, f32[32,256]{1,0:T(8,128)S(1)}, f32[32]{0:T(128)}, ...), condition=%wide.region_1.2_spmd, body=%wide.region_0.1_spmd.sunk | while | flops 20971524 | bytes 125121 | solution.py:47
  25.0 6.0 fusion.62
  34.9 6.0 fusion.62
  44.8 6.0 fusion.62
  54.8 6.0 fusion.62
  64.7 6.0 fusion.62
  74.6 6.0 fusion.62
  84.5 6.0 fusion.62
  94.4 6.0 fusion.62
  104.4 6.0 fusion.62
  114.3 6.0 fusion.62
  124.2 6.0 fusion.62
  134.1 6.0 fusion.62
  144.0 6.0 fusion.62
  154.0 6.0 fusion.62
  163.9 6.0 fusion.62
  183.7 6.0 fusion.62
  193.6 6.0 fusion.62
  213.5 6.0 fusion.62
  243.2 6.0 fusion.62
  263.1 6.0 fusion.62
  273.0 6.0 fusion.62
  292.8 6.0 fusion.62
  302.7 6.0 fusion.62
  322.6 6.0 fusion.62
  338.6 6.3 all_to_all.38
  345.7 7.9 %gather_fusion.1 = bf16[256,4096]{1,0:T(8,128)(2,1)} fusion(bf16[512,4096]{1,0:T(8,128)(2,1)} %param.15, s32[1024]{0:T(1024)S(1)} %pad_clamp_fusion), kind=kCustom, calls=%fused_computation.1 | custom fusion | bytes 4195328 | tf_op jit(solution)/shard_map/jit(_take)/gather | solution.py:51
  354.6 13.4 %all_gather.10 = bf16[64,256]{0,1:T(8,128)(2,1)S(1)} all-gather(bf16[64,64]{0,1:T(8,128)(2,1)S(1)} %copy.42), channel_id=1, replica_groups=mesh['group'=2,'gene'=4,'lat'=2,'sub'=2] {'gene'}, dimensions={1}, use_global_device_ids=true | all-gather | bytes 40960 | tf_op jit(solution)/shard_map/all_gather | solution.py:50
  371.9 20.6 %reduce-scatter.9.cloned.1.call-done = f32[64,64]{1,0:T(8,128)} async-done(((f32[256,64]{1,0:T(8,128)}), f32[64,64]{1,0:T(8,128)}) %reduce-scatter.9.cloned.1.call-update) | async-done | bytes 16400
  402.4 294.5 %while.21 = (s32[]{:T(128)}, f32[32,4096]{1,0:T(8,128)}, f32[32,256]{1,0:T(8,128)S(1)}, f32[32]{0:T(128)S(1)}, f32[2,256]{1,0:T(2,128)S(1)}, /*index=5*/f32[32,2...) while((s32[]{:T(128)}, f32[32,4096]{1,0:T(8,128)}, ...), condition=%wide.region_6.7_spmd, body=%wide.region_5.6_spmd.sunk | while | flops 20971524 | bytes 154825 | solution.py:76
  696.9 36.0 %all-reduce.5.cloned.1.call-done = f32[32,4096]{1,0:T(8,128)} async-done(((f32[32,4096]{1,0:T(8,128)}), f32[32,4096]{1,0:T(8,128)}) %all-reduce.5.cloned.1.call-update) | async-done | bytes 524304 | tf_op jit(solution)/shard_map/psum | solution.py:77
  (406 shorter events, 403.3 us)
Async XLA Ops:
  7.2 360.8 %copy-start = (bf16[64,4096]{1,0:T(8,128)(2,1)S(1)}, bf16[64,4096]{1,0:T(8,128)(2,1)}, u32[]{:S(2)}) copy-start(bf16[64,4096]{1,0:T(8,128)(2,1)} %param.20) | copy-start | bytes 1572868
  7.2 346.4 %reduce-scatter.7.cloned.1.call-start = ((), (), s32[]{:S(2)}) async-start(), calls=%async_computation.6 | async-start | bytes 98304
  338.5 15.1 %copy-start.1 = (f32[32,2,4096]{2,1,0:T(2,128)}, f32[32,2,4096]{2,1,0:T(2,128)S(1)}, u32[]{:S(2)}) copy-start(f32[32,2,4096]{2,1,0:T(2,128)S(1)} %get-tuple-element.290) | copy-start | bytes 3145732
  345.6 22.3 %copy-start.2 = (f32[4096]{0:T(1024)S(1)}, f32[4096]{0:T(1024)}, u32[]{:S(2)}) copy-start(f32[4096]{0:T(1024)} %param.21) | copy-start | bytes 49156
  345.6 46.9 %reduce-scatter.9.cloned.1.call-start = ((), (), s32[]{:S(2)}) async-start(), calls=%async_computation.7 | async-start | bytes 163840
  370.3 32.1 %copy-start.3 = (f32[32]{0:T(128)S(1)}, f32[32]{0:T(128)}, u32[]{:S(2)}) copy-start(f32[32]{0:T(128)} %get-tuple-element.303) | copy-start | bytes 388
  370.3 32.1 %copy-start.4 = (f32[32]{0:T(128)S(1)}, f32[32]{0:T(128)}, u32[]{:S(2)}) copy-start(f32[32]{0:T(128)} %get-tuple-element.304) | copy-start | bytes 388
  395.2 7.2 all-to-all-start.1
  398.5 298.4 %all-reduce.3.cloned.1.call-start = ((), (), s32[]{:S(2)}) async-start(), calls=%async_computation.4 | async-start | bytes 2097152 | tf_op jit(solution)/shard_map/psum | solution.py:60
  400.2 332.7 %all-reduce.5.cloned.1.call-start = ((), (), s32[]{:S(2)}) async-start(), calls=%async_computation.5 | async-start | bytes 1048576 | tf_op jit(solution)/shard_map/psum | solution.py:77
Sparse Core Ops, SparseCore 0:
  345.7 7.8 reduce-scatter.6
  372.0 20.4 reduce-scatter.8
  402.2 34.9 all-reduce.2
  697.0 35.8 all-reduce.4
where the time goes:
time: 750 us; the launch traced here: 744 us
  matrix products  325 us (43%)
  local copies, waits for them, and re-layouts  220 us (29%)
  loops' own time  90 us (12%)
  waiting for transfers between devices  58.8 us (8%)
  blocking collectives  30.4 us (4%)
  between operations  13.9 us (2%)
    dot_general x32, matrix products, forward(): jnp.dot(kernel_tile(kernel_xy, points, length, height), weights, precisio...  191 us
    dot_general x32, matrix products, backward(): jnp.dot(gradient, kernel_tile(kernel_xy, points, length, height), precisi...  129 us
    dynamic_slice x128, local copies, waits for them, and re-layouts, on_device(): local_latent = lax.map(forward, (moved, ind_weights, lengthscale, variance))  119 us
    dynamic_update_slice x32, local copies, waits for them, and re-layouts, on_device(): lax.map(backward, (moved, latent_grad, lengthscale, variance))  51.7 us
    another operation x1, loops' own time, on_device(): lax.map(backward, (moved, latent_grad, lengthscale, variance))  46 us
    another operation x1, loops' own time, on_device(): local_latent = lax.map(forward, (moved, ind_weights, lengthscale, variance))  44 us
    psum x1, waiting for transfers between devices, on_device(): grad_inducing = lax.psum(partial_inducing, 'gene')  36 us
    slice x128, local copies, waits for them, and re-layouts, kernel_tile(): delta_x = cell_xy[0][:, None] - points[0][None, :]  29.4 us
  transfers between devices with their start and end apart: 5, of which 3 were waited for; matrix products, arithmetic and copies ran while one was open for 35% of the time, Pallas kernels for 0%

commit v1 on v0

v1 whole, which is shorter than its diff:
```python
import functools
import math

import jax
import jax.numpy as jnp
from jax import lax
from jax.experimental import pallas as pl
from jax.experimental.pallas import tpu as pltpu
from jax.sharding import PartitionSpec as P

F32 = jnp.float32
BF16 = jnp.bfloat16
GROUP = 8
DEPTH = 24
SPARE = 21
CENTER = 0.5


def pieces(value):
    high = value.astype(BF16).astype(F32)
    rest = value - high
    middle = rest.astype(BF16).astype(F32)
    low = (rest - middle).astype(BF16).astype(F32)
    return high, middle, low


def pieces_outside(value):
    high = lax.reduce_precision(value, 8, 7)
    rest = value - high
    middle = lax.reduce_precision(rest, 8, 7)
    low = lax.reduce_precision(rest - middle, 8, 7)
    return high, middle, low


LEFT = (0, 0, 1, 1, 0, 2)
RIGHT = (0, 1, 0, 1, 2, 0)


def cell_features(xy):
    x, y = xy[0] - CENTER, xy[1] - CENTER
    px, py, pn = pieces_outside(x), pieces_outside(y), pieces_outside(x * x + y * y)
    one, zero = jnp.ones_like(x), jnp.zeros_like(x)
    columns = [px[i] for i in LEFT] + [py[i] for i in LEFT] + [pn[i] for i in LEFT]
    columns += [one] * 3 + [zero] * (DEPTH - SPARE)
    return jnp.stack(columns, axis=1).astype(BF16)


def point_features(points_ref, length_ref, extra, table_ref):
    length = length_ref[...]
    scale = 0.5 / (length * length)
    x = points_ref[0] - CENTER
    y = points_ref[1] - CENTER
    px = pieces(x * (2.0 * scale))
    py = pieces(y * (2.0 * scale))
    ps = pieces(jnp.broadcast_to(-scale, x.shape))
    pn = pieces((x * x + y * y) * -scale)
    rows = [px[i] for i in RIGHT] + [py[i] for i in RIGHT] + [ps[i] for i in RIGHT]
    rows += list(pn) + [extra] + [jnp.zeros_like(x)] * (DEPTH - SPARE - 1)
    for place, row in enumerate(rows):
        for lane in range(GROUP):
            table_ref[lane, place : place + 1, :] = row[lane : lane + 1, :]


def forward_body(tile, feat_ref, points_ref, weight_ref, length_ref, height_ref, out_ref, table_ref, wide_ref):
    point_features(points_ref, length_ref, weight_ref[...], table_ref)
    feat = feat_ref[...]
    count = weight_ref.shape[1]

    def one(j, carry):
        total = jnp.zeros((feat.shape[0], 128), F32)
        for start in range(0, count, tile):
            part = table_ref[j, :, start : start + tile].astype(BF16)
            value = jnp.exp(jnp.dot(feat, part, preferred_element_type=F32))
            for lane in range(0, tile, 128):
                w = table_ref[j, SPARE : SPARE + 1, start + lane : start + lane + 128]
                total = total + value[:, lane : lane + 128] * w
        wide_ref[j] = total
        return carry

    lax.fori_loop(0, GROUP, one, 0)
    for j in range(GROUP):
        total = jnp.sum(wide_ref[j].T, axis=0, keepdims=True)
        out_ref[j : j + 1, :] = total * height_ref[j : j + 1, :]


def backward_body(
    tile, feat_ref, points_ref, grad_ref, length_ref, height_ref, out_ref, table_ref, wide_ref, sum_ref
):
    count = points_ref.shape[2]
    point_features(points_ref, length_ref, jnp.zeros((GROUP, count), F32), table_ref)
    feat = feat_ref[...]
    rows = feat.shape[0]
    grad = (grad_ref[...] * height_ref[...]).T
    for j in range(GROUP):
        wide_ref[j] = jnp.broadcast_to(grad[:, j : j + 1], (rows, 128))

    def one(j, carry):
        for start in range(0, count, tile):
            part = table_ref[j, :, start : start + tile].astype(BF16)
            value = jnp.exp(jnp.dot(feat, part, preferred_element_type=F32))
            for lane in range(0, tile, 128):
                term = value[:, lane : lane + 128] * wide_ref[j]
                sum_ref[j, :, start + lane : start + lane + 128] = jnp.sum(
                    term.reshape(rows // 8, 8, 128), axis=0
                )
        return carry

    lax.fori_loop(0, GROUP, one, 0)
    for j in range(GROUP):
        out_ref[j : j + 1, :] = jnp.sum(sum_ref[j], axis=0, keepdims=True)


def middle_body(scale, index_ref, expr_ref, latent_ref, mixing_ref, noise_ref, mix_out_ref, cell_out_ref):
    rows = index_ref.shape[0]
    table = expr_ref.shape[0]
    pick = (lax.broadcasted_iota(jnp.int32, (rows, table), 1) == index_ref[...]).astype(F32).astype(BF16)
    observed = jnp.dot(pick, expr_ref[...], preferred_element_type=F32)
    latent = latent_ref[...]
    mixing = mixing_ref[...]
    predicted = lax.dot_general(latent, mixing, (((0,), (0,)), ((), ())), preferred_element_type=F32)
    weighted = (noise_ref[...] * (observed - predicted)).astype(BF16)
    mix_out_ref[...] = scale * jnp.dot(latent, weighted, preferred_element_type=F32)

    @pl.when(pl.program_id(0) == 0)
    def _():
        cell_out_ref[...] = jnp.zeros_like(cell_out_ref)

    cell_out_ref[...] += scale * lax.dot_general(
        mixing, weighted, (((1,), (1,)), ((), ())), preferred_element_type=F32
    )


def products(body, out_shape, scratch, feat, points, other, length, height):
    lats, count = points.shape[1], points.shape[2]
    rows = feat.shape[0]
    tile = min(256, count)
    work = rows * lats * count
    return pl.pallas_call(
        functools.partial(body, tile),
        grid=(lats // GROUP,),
        in_specs=[
            pl.BlockSpec((rows, DEPTH), lambda i: (0, 0)),
            pl.BlockSpec((2, GROUP, count), lambda i: (0, i, 0)),
            pl.BlockSpec((GROUP, other.shape[1]), lambda i: (i, 0)),
            pl.BlockSpec((GROUP, 1), lambda i: (i, 0)),
            pl.BlockSpec((GROUP, 1), lambda i: (i, 0)),
        ],
        out_specs=pl.BlockSpec((GROUP, out_shape[1]), lambda i: (i, 0)),
        out_shape=jax.ShapeDtypeStruct(out_shape, F32),
        scratch_shapes=[pltpu.VMEM((GROUP, DEPTH, count), F32), *scratch],
        cost_estimate=pl.CostEstimate(
            flops=2 * DEPTH * work, transcendentals=work, bytes_accessed=12 * lats * count
        ),
        compiler_params=pltpu.CompilerParams(vmem_limit_bytes=40 * 2**20),
    )(feat, points, other, length[:, None], height[:, None])


def middle(scale, cell_index, expr_table, latent, mixing, noise_prec):
    rows = cell_index.shape[0]
    table, genes = expr_table.shape
    lats = latent.shape[0]
    tile = min(512, genes)
    return pl.pallas_call(
        functools.partial(middle_body, scale),
        grid=(genes // tile,),
        in_specs=[
            pl.BlockSpec((rows, 1), lambda i: (0, 0)),
            pl.BlockSpec((table, tile), lambda i: (0, i)),
            pl.BlockSpec((lats, rows), lambda i: (0, 0)),
            pl.BlockSpec((lats, tile), lambda i: (0, i)),
            pl.BlockSpec((1, tile), lambda i: (0, i)),
        ],
        out_specs=[
            pl.BlockSpec((lats, tile), lambda i: (0, i)),
            pl.BlockSpec((lats, rows), lambda i: (0, 0)),
        ],
        out_shape=[
            jax.ShapeDtypeStruct((lats, genes), F32),
            jax.ShapeDtypeStruct((lats, rows), F32),
        ],
        compiler_params=pltpu.CompilerParams(vmem_limit_bytes=40 * 2**20),
    )(cell_index[:, None], expr_table, latent, mixing, noise_prec[None, :])


def on_device(
    cell_index,
    coords_table,
    expr_table,
    inducing,
    ind_weights,
    lengthscale,
    variance,
    mixing,
    noise_prec,
):
    gene_count = lax.axis_size("gene")
    lat_count = lax.axis_size("lat")
    sub_count = lax.axis_size("sub")
    bat_rows = cell_index.shape[0]
    per_block = bat_rows // gene_count
    block_count = lat_count * sub_count
    gene_place = lax.axis_index("gene")
    mine = lax.dynamic_slice_in_dim(cell_index, gene_place * per_block, per_block, 0)
    picks = mine[:, None] == jnp.arange(coords_table.shape[1], dtype=mine.dtype)[None, :]
    local_xy = jnp.sum(jnp.where(picks[None], coords_table[:, None, :], 0.0), axis=2)
    kernel_xy = lax.all_gather(local_xy, ("lat", "sub"), axis=1, tiled=True)
    feat = cell_features(kernel_xy)
    rows = feat.shape[0]
    lats, count = ind_weights.shape
    local_latent = products(
        forward_body, (lats, rows), [pltpu.VMEM((GROUP, rows, 128), F32)], feat, inducing, ind_weights, lengthscale, variance
    )
    swapped = lax.all_to_all(local_latent, "lat", split_axis=1, concat_axis=0, tiled=True)
    summed = lax.psum_scatter(swapped, "sub", scatter_dimension=1, tiled=True).astype(BF16)
    latent = lax.all_gather(summed, "gene", axis=1, tiled=True)
    grad_scale = -1.0 / math.sqrt(bat_rows * block_count)
    mixing_term, cell_term = middle(grad_scale, cell_index, expr_table, latent, mixing, noise_prec)
    grad_mixing = lax.psum(mixing_term, ("lat", "sub"))
    shared = lax.psum_scatter(cell_term, "gene", scatter_dimension=1, tiled=True)
    paired = lax.all_gather(shared, "sub", axis=1, tiled=True)
    latent_grad = lax.all_to_all(paired, "lat", split_axis=0, concat_axis=1, tiled=True)
    scratch = [pltpu.VMEM((GROUP, rows, 128), F32), pltpu.VMEM((GROUP, 8, count), F32)]
    partial_inducing = products(
        backward_body, (lats, count), scratch, feat, inducing, latent_grad, lengthscale, variance
    )
    grad_inducing = lax.psum(partial_inducing, "gene")
    return (grad_mixing, grad_inducing)


def solution(mesh):
    in_specs = (
        P(("group", "lat", "sub")),
        P("group", ("lat", "sub")),
        P(("group", "lat", "sub"), "gene"),
        P("group", "lat", "sub"),
        P(("group", "lat"), "sub"),
        P(("group", "lat")),
        P(("group", "lat")),
        P("group", "gene"),
        P(("group", "gene")),
    )
    out_specs = (P("group", "gene"), P(("group", "lat"), "sub"))
    return jax.shard_map(
        on_device, mesh=mesh, in_specs=in_specs, out_specs=out_specs, check_vma=False
    )
```

time: 750 us -> 199 us (0.27)
  matrix products: 325 us -> 0 us
  local copies, waits for them, and re-layouts: 220 us -> 13.8 us
  loops' own time: 90 us -> 0 us
  Pallas kernels: 0 us -> 64.5 us
  waiting for transfers between devices: 58.8 us -> 70 us
    dot_general x67 -> x0, matrix products: 325 us -> none  [the longest x32 191 us: forward(): jnp.dot(kernel_tile(kernel_xy, points, length, height), weights, precisio...]
    dynamic_slice x129 -> x1, local copies, waits for them, and re-layouts: 119 us -> 0.75 us  [on_device(): lax.dynamic_slice_in_dim(cell_index, gene_place * per_block, per_block, 0)]
    another operation x2 -> x0, loops' own time: 90 us -> none  [the longest x1 46 us: on_device(): lax.map(backward, (moved, latent_grad, lengthscale, variance))]
    pallas_call x0 -> x3, Pallas kernels: none -> 64.5 us  [the longest x2 56.6 us: products(): pl.pallas_call(functools.partial(body, tile), grid=(lats // GROUP,), in_s...]
    dynamic_update_slice x64 -> x0, local copies, waits for them, and re-layouts: 52.9 us -> none  [the longest x32 51.7 us: on_device(): lax.map(backward, (moved, latent_grad, lengthscale, variance))]
    slice x128 -> x0, local copies, waits for them, and re-layouts: 29.4 us -> none  [kernel_tile(): delta_x = cell_xy[0][:, None] - points[0][None, :]]
    gather x2 -> x0, local copies, waits for them, and re-layouts: 8.67 us -> none  [the longest x1 7.94 us: on_device(): observed = jnp.take(expr_table, cell_index, axis=0)]
    unnamed x6, waiting for transfers between devices: 20.6 us -> 28.3 us
  transfers between devices with their start and end apart: 5 -> 4, of which waited for: 3 -> 3; matrix products, arithmetic and copies ran while one was open for 35% -> 0% of each run, Pallas kernels for 0% -> 15%
where the time goes in v1:
time: 199 us; the launch traced here: 198 us
  waiting for transfers between devices  70 us (35%)
  Pallas kernels  64.5 us (32%)
  blocking collectives  35.1 us (18%)
  between operations  13.9 us (7%)
  local copies, waits for them, and re-layouts  13.8 us (7%)
    pallas_call x2, Pallas kernels, products(): pl.pallas_call(functools.partial(body, tile), grid=(lats // GROUP,), in_s...  56.6 us
    psum x1, waiting for transfers between devices, on_device(): grad_inducing = lax.psum(partial_inducing, 'gene')  41.7 us
    unnamed x6, waiting for transfers between devices  28.3 us
    all_gather x1, blocking collectives, on_device(): latent = lax.all_gather(summed, 'gene', axis=1, tiled=True)  13.4 us
    unnamed x20, local copies, waits for them, and re-layouts  11 us
    pallas_call x1, Pallas kernels, middle(): pl.pallas_call(functools.partial(middle_body, scale), grid=(genes // tile...  7.9 us
    all_to_all x1, blocking collectives, on_device(): lax.all_to_all(local_latent, 'lat', split_axis=1, concat_axis=0, tiled=True)  7.03 us
    all_to_all x1, blocking collectives, on_device(): lax.all_to_all(paired, 'lat', split_axis=0, concat_axis=1, tiled=True)  6.59 us
  transfers between devices with their start and end apart: 4, of which 3 were waited for; matrix products, arithmetic and copies ran while one was open for 0% of the time, Pallas kernels for 15%

profile of v1, /device:TPU:0, one launch (start us, length us, event | category | flops | bytes accessed | tf_op | source)
XLA Modules:
  0.0 198.4 jit_solution(17748286052401506881)
XLA Ops:
  7.2 0.7 copy.85.length_ref
  8.0 0.7 copy.86.height_ref
  8.7 0.8 dynamic_slice.3
  9.4 0.1 iota_compare_fusion
  9.5 0.8 select_reduce_fusion
  10.3 6.0 %all-gather = f32[4,64,2]{1,2,0:T(2,128)S(1)} all-gather(f32[1,64,2]{1,2,0:T(2,128)S(1)} %bitcast.59), channel_id=1, replica_groups=mesh['group'=2,'gene'=4,'lat'=2,'sub'=2] {'lat','sub'}, dimensions={0}, use_global_device_ids=true | all-gather | bytes 2560 | tf_op jit(solution)/shard_map/all_gather | solution.py:206
  16.3 0.1 reshape.148
  16.5 0.1 stack.9
  16.6 0.1 copy.84.feat_ref
  16.7 1.2 copy-done.3
  18.0 1.0 copy-done.5
  19.0 27.7 %shard_map.104 = f32[32,256]{1,0:T(8,128)S(1)} custom-call(bf16[256,24]{1,0:T(8,128)(2,1)S(1)} %copy.84.feat_ref, f32[2,32,4096]{2,1,0:T(8,128)S(1)} %copy-done.3, f32[32,4096]{1,0:T(8,128)S(1)} %copy-done.5, f32[32,1]{1,0:T(8,128)S(1)} %copy.85.length_ref, f32[32,1]{1,0:T(8,128)S(1)} %copy.86.height_ref), custom_call_target="tpu_custom_call" | custom-call | flops 1610612736 | bytes 1572864 | tf_op jit(solution)/shard_map/pallas_call | solution.py:138
  46.7 7.0 %all_to_all.38 = f32[32,2,128]{2,0,1:T(8,128)S(1)} all-to-all(f32[32,2,128]{2,0,1:T(8,128)S(1)} %copy_bitcast_fusion.1), channel_id=1, replica_groups=mesh['group'=2,'gene'=4,'lat'=2,'sub'=2] {'lat'}, dimensions={1} | all-to-all | bytes 65536 | tf_op jit(solution)/shard_map/all_to_all | solution.py:213
  53.8 0.7 copy.97
  54.6 0.1 copy.89.index_ref
  54.7 7.8 %reduce-scatter.7.cloned.1.call-done = f32[64,64]{1,0:T(8,128)} async-done(((f32[128,64]{1,0:T(8,128)}), f32[64,64]{1,0:T(8,128)}) %reduce-scatter.7.cloned.1.call-update) | async-done | bytes 16400
  62.5 0.8 copy.98
  63.4 0.1 copy.88
  63.5 13.4 %all_gather.10 = bf16[64,256]{0,1:T(8,128)(2,1)S(1)} all-gather(bf16[64,64]{0,1:T(8,128)(2,1)S(1)} %copy.88), channel_id=1, replica_groups=mesh['group'=2,'gene'=4,'lat'=2,'sub'=2] {'gene'}, dimensions={1}, use_global_device_ids=true | all-gather | bytes 40960 | tf_op jit(solution)/shard_map/all_gather | solution.py:215
  76.9 0.1 copy.90.latent_ref
  77.0 2.2 %copy-done = bf16[512,4096]{1,0:T(8,128)(2,1)S(1)} copy-done((bf16[512,4096]{1,0:T(8,128)(2,1)S(1)}, bf16[512,4096]{1,0:T(8,128)(2,1)}, u32[]{:S(2)}) %copy-start) | copy-done | bytes 4194328
  79.2 7.9 %shard_map.105 = (f32[64,4096]{1,0:T(8,128)}, f32[64,256]{1,0:T(8,128)S(1)}) custom-call(s32[256,1]{1,0:T(8,128)S(1)} %copy.89.index_ref, bf16[512,4096]{1,0:T(8,128)(2,1)S(1)} %copy-done, bf16[64,256]{1,0:T(8,128)(2,1)S(1)} %copy.90.latent_ref, bf16[64,4096]{1,0:T(8,128)(2,1)S(1)} %copy-done.1, f32[1,4096]{1,0:T(1,128)S(1)} %bitcast.51), custom_call_target="tpu_custom_call" | custom-call | tf_op jit(solution)/shard_map/pallas_call | solution.py:163
  87.1 0.8 copy.99
  87.9 0.7 all-reduce.3.cloned.1.call-update
  88.6 19.8 %reduce-scatter.9.cloned.1.call-done = f32[64,64]{1,0:T(8,128)} async-done(((f32[256,64]{1,0:T(8,128)}), f32[64,64]{1,0:T(8,128)}) %reduce-scatter.9.cloned.1.call-update) | async-done | bytes 16400
  108.4 2.1 %all_gather.11 = f32[64,128]{0,1:T(8,128)S(1)} all-gather(f32[64,64]{0,1:T(8,128)} %bitcast.56), channel_id=1, replica_groups=mesh['group'=2,'gene'=4,'lat'=2,'sub'=2] {'sub'}, dimensions={1}, use_global_device_ids=true | all-gather | bytes 49152 | tf_op jit(solution)/shard_map/all_gather | solution.py:220
  110.5 0.1 copy.92
  110.6 6.6 %all_to_all.39 = f32[2,32,128]{2,1,0:T(8,128)S(1)} all-to-all(f32[2,32,128]{2,1,0:T(8,128)S(1)} %bitcast.55), channel_id=1, replica_groups=mesh['group'=2,'gene'=4,'lat'=2,'sub'=2] {'lat'}, dimensions={0} | all-to-all | bytes 65536 | tf_op jit(solution)/shard_map/all_to_all | solution.py:221
  117.2 28.9 %shard_map.106 = f32[32,4096]{1,0:T(8,128)} custom-call(bf16[256,24]{1,0:T(8,128)(2,1)S(1)} %copy.84.feat_ref, f32[2,32,4096]{2,1,0:T(8,128)S(1)} %copy-done.4, f32[32,256]{1,0:T(8,128)S(1)} %copy_bitcast_fusion.grad_ref, f32[32,1]{1,0:T(8,128)S(1)} %copy.85.length_ref, f32[32,1]{1,0:T(8,128)S(1)} %copy.86.height_ref), custom_call_target="tpu_custom_call" | custom-call | flops 1610612736 | bytes 1572864 | tf_op jit(solution)/shard_map/pallas_call | solution.py:138
  146.1 41.7 %all-reduce.5.cloned.1.call-done = f32[32,4096]{1,0:T(8,128)} async-done(((f32[32,4096]{1,0:T(8,128)}), f32[32,4096]{1,0:T(8,128)}) %all-reduce.5.cloned.1.call-update) | async-done | bytes 524304 | tf_op jit(solution)/shard_map/psum | solution.py:226
  187.8 2.3 %copy.107 = f32[64,4096]{1,0:T(8,128)} copy(f32[64,4096]{1,0:T(8,128)} %all-reduce.3.cloned.1.call-done) | data formatting | bytes 2097152
  190.0 1.9 copy.108
  (28 shorter events, 0.3 us)
Async XLA Ops:
  7.2 55.4 %reduce-scatter.7.cloned.1.call-start = ((), (), s32[]{:S(2)}) async-start(), calls=%async_computation.6 | async-start | bytes 98304
  16.7 1.2 copy-start.3
  18.0 1.0 copy-start.5
  19.0 35.6 %copy-start.6 = (s32[256]{0:T(256)S(1)}, s32[256]{0:T(256)}, u32[]{:S(2)}) copy-start(s32[256]{0:T(256)} %param.9) | copy-start | bytes 3076
  19.0 58.0 %copy-start.1 = (bf16[64,4096]{1,0:T(8,128)(2,1)S(1)}, bf16[64,4096]{1,0:T(8,128)(2,1)}, u32[]{:S(2)}) copy-start(bf16[64,4096]{1,0:T(8,128)(2,1)} %mixing_ref.1) | copy-start | bytes 1572868
  19.0 58.0 %copy-start.2 = (f32[4096]{0:T(1024)S(1)}, f32[4096]{0:T(1024)}, u32[]{:S(2)}) copy-start(f32[4096]{0:T(1024)} %param.17) | copy-start | bytes 49156
  19.0 98.2 %copy-start.4 = (f32[2,32,4096]{2,1,0:T(8,128)S(1)}, f32[2,32,4096]{2,1,0:T(8,128)}, u32[]{:S(2)}) copy-start(f32[2,32,4096]{2,1,0:T(8,128)} %points_ref.3) | copy-start | bytes 3145732
  54.5 53.9 %reduce-scatter.9.cloned.1.call-start = ((), (), s32[]{:S(2)}) async-start(), calls=%async_computation.7 | async-start | bytes 163840
  77.0 2.2 %copy-start = (bf16[512,4096]{1,0:T(8,128)(2,1)S(1)}, bf16[512,4096]{1,0:T(8,128)(2,1)}, u32[]{:S(2)}) copy-start(bf16[512,4096]{1,0:T(8,128)(2,1)} %expr_ref.1) | copy-start | bytes 12582916
  87.9 58.2 %all-reduce.3.cloned.1.call-start = ((), (), s32[]{:S(2)}) async-start(), calls=%async_computation.4 | async-start | bytes 2097152 | tf_op jit(solution)/shard_map/psum | solution.py:218
  88.6 99.2 %all-reduce.5.cloned.1.call-start = ((), (), s32[]{:S(2)}) async-start(), calls=%async_computation.5 | async-start | bytes 1048576 | tf_op jit(solution)/shard_map/psum | solution.py:226
Sparse Core Ops, SparseCore 0:
  54.7 7.8 reduce-scatter.6
  88.0 20.4 reduce-scatter.8
  111.4 34.4 all-reduce.2
  148.7 39.0 all-reduce.4

commit v2 on v1

--- a/solution.py
+++ b/solution.py
@@ -80,7 +80,10 @@
     lax.fori_loop(0, GROUP, one, 0)
     for j in range(GROUP):
         total = jnp.sum(wide_ref[j].T, axis=0, keepdims=True)
-        out_ref[j : j + 1, :] = total * height_ref[j : j + 1, :]
+        total = total * height_ref[j : j + 1, :]
+        blocks, _, width = out_ref.shape
+        for block in range(blocks):
+            out_ref[block, j : j + 1, :] = total[:, block * width : (block + 1) * width]
 
 
 def backward_body(
@@ -110,7 +113,7 @@
         out_ref[j : j + 1, :] = jnp.sum(sum_ref[j], axis=0, keepdims=True)
 
 
-def middle_body(scale, index_ref, expr_ref, latent_ref, mixing_ref, noise_ref, mix_out_ref, cell_out_ref):
+def middle_body(scale, index_ref, expr_ref, latent_ref, mixing_ref, noise_ref, mix_out_ref, chunk_ref, cell_ref):
     rows = index_ref.shape[0]
     table = expr_ref.shape[0]
     pick = (lax.broadcasted_iota(jnp.int32, (rows, table), 1) == index_ref[...]).astype(F32).astype(BF16)
@@ -123,11 +126,146 @@
 
     @pl.when(pl.program_id(0) == 0)
     def _():
-        cell_out_ref[...] = jnp.zeros_like(cell_out_ref)
-
-    cell_out_ref[...] += scale * lax.dot_general(
+        cell_ref[...] = jnp.zeros_like(cell_ref)
+
+    cell_ref[...] += scale * lax.dot_general(
         mixing, weighted, (((1,), (1,)), ((), ())), preferred_element_type=F32
     )
+
+    @pl.when(pl.program_id(0) == pl.num_programs(0) - 1)
+    def _():
+        genes, lats, depth, width = chunk_ref.shape
+        for gene in range(genes):
+            for lat in range(lats):
+                chunk_ref[gene, lat] = cell_ref[
+                    lat * depth : (lat + 1) * depth, gene * width : (gene + 1) * width
+                ]
+
+
+AXES = ("gene", "lat", "sub")
+
+
+def place_of(rank, sizes):
+    return rank // (sizes[1] * sizes[2]), rank // sizes[2] % sizes[1], rank % sizes[2]
+
+
+def greet(ranks):
+    barrier = pltpu.get_barrier_semaphore()
+    for device in ranks:
+        pl.semaphore_signal(barrier, inc=1, device_id=device, device_id_type=pl.DeviceIdType.MESH)
+    pl.semaphore_wait(barrier, len(ranks))
+
+
+def exchange_body(sizes, chunk_of, finish, send_ref, out_ref, recv_ref, send_sem, recv_sem, own_sem):
+    total = sizes[0] * sizes[1] * sizes[2]
+    place = tuple(lax.axis_index(axis) for axis in AXES)
+    me = (place[0] * sizes[1] + place[1]) * sizes[2] + place[2]
+    peers = [place_of(lax.rem(me + k, total), sizes) for k in range(1, total)]
+    greet([dict(zip(AXES, peer)) for peer in peers])
+    copies = []
+    for k, peer in enumerate(peers):
+        copy = pltpu.make_async_remote_copy(
+            src_ref=send_ref.at[chunk_of(peer)],
+            dst_ref=recv_ref.at[me],
+            send_sem=send_sem.at[k],
+            recv_sem=recv_sem.at[k],
+            device_id=dict(zip(AXES, peer)),
+            device_id_type=pl.DeviceIdType.MESH,
+        )
+        copy.start()
+        copies.append(copy)
+    own = pltpu.make_async_copy(send_ref.at[chunk_of(place)], recv_ref.at[me], own_sem)
+    own.start()
+    own.wait()
+    for copy in copies:
+        copy.wait()
+    finish(recv_ref, out_ref)
+
+
+def exchange(sizes, chunk_of, finish, out, collective_id, send):
+    total = sizes[0] * sizes[1] * sizes[2]
+    return pl.pallas_call(
+        functools.partial(exchange_body, sizes, chunk_of, finish),
+        in_specs=[pl.BlockSpec(memory_space=pltpu.VMEM)],
+        out_specs=pl.BlockSpec(memory_space=pltpu.VMEM),
+        out_shape=out,
+        scratch_shapes=[
+            pltpu.VMEM((total, *send.shape[1:]), F32),
+            pltpu.SemaphoreType.DMA((total - 1,)),
+            pltpu.SemaphoreType.DMA((total - 1,)),
+            pltpu.SemaphoreType.DMA,
+        ],
+        compiler_params=pltpu.CompilerParams(collective_id=collective_id, has_side_effects=True),
+    )(send)
+
+
+def gene_sum_body(genes, x_ref, out_ref, recv_ref, sum_ref, all_ref, send_sem, recv_sem, back_sem, full_sem):
+    me = lax.axis_index("gene")
+    width = sum_ref.shape[1]
+    peers = [lax.rem(me + k, genes) for k in range(1, genes)]
+    greet([{"gene": peer} for peer in peers])
+
+    def columns(place):
+        return pl.ds(pl.multiple_of(place * width, 128), width)
+
+    copies = []
+    for k, peer in enumerate(peers):
+        copy = pltpu.make_async_remote_copy(
+            src_ref=x_ref.at[:, columns(peer)],
+            dst_ref=recv_ref.at[k],
+            send_sem=send_sem.at[k],
+            recv_sem=recv_sem.at[k],
+            device_id={"gene": peer},
+            device_id_type=pl.DeviceIdType.MESH,
+        )
+        copy.start()
+        copies.append(copy)
+    for copy in copies:
+        copy.wait()
+    value = x_ref[:, columns(me)]
+    for k in range(genes - 1):
+        value = value + recv_ref[k]
+    sum_ref[...] = value
+    backs = []
+    for k, peer in enumerate(peers):
+        copy = pltpu.make_async_remote_copy(
+            src_ref=sum_ref,
+            dst_ref=all_ref.at[k],
+            send_sem=back_sem.at[k],
+            recv_sem=full_sem.at[k],
+            device_id={"gene": peer},
+            device_id_type=pl.DeviceIdType.MESH,
+        )
+        copy.start()
+        backs.append(copy)
+    out_ref[:, columns(me)] = value
+    for k, copy in enumerate(backs):
+        copy.wait()
+        out_ref[:, columns(lax.rem(me + genes - 1 - k, genes))] = all_ref[k]
+
+
+def gene_sum(genes, collective_id, x):
+    rows, count = x.shape
+    width = count // genes
+    sems = pltpu.SemaphoreType.DMA((genes - 1,))
+    return pl.pallas_call(
+        functools.partial(gene_sum_body, genes),
+        in_specs=[pl.BlockSpec(memory_space=pltpu.VMEM)],
+        out_specs=pl.BlockSpec(memory_space=pltpu.VMEM),
+        out_shape=jax.ShapeDtypeStruct(x.shape, F32),
+        scratch_shapes=[
+            pltpu.VMEM((genes - 1, rows, width), F32),
+            pltpu.VMEM((rows, width), F32),
+            pltpu.VMEM((genes - 1, rows, width), F32),
+            sems,
+            sems,
+            sems,
+            sems,
+        ],
+        compiler_params=pltpu.CompilerParams(
+            collective_id=collective_id, has_side_effects=True, vmem_limit_bytes=40 * 2**20
+        ),
+    )(x)
 
 
 def products(body, out_shape, scratch, feat, points, other, length, height):
@@ -145,7 +283,9 @@
             pl.BlockSpec((GROUP, 1), lambda i: (i, 0)),
             pl.BlockSpec((GROUP, 1), lambda i: (i, 0)),
         ],
-        out_specs=pl.BlockSpec((GROUP, out_shape[1]), lambda i: (i, 0)),
+        out_specs=pl.BlockSpec(
+            (*out_shape[:-2], GROUP, out_shape[-1]), lambda i: (*(0 for _ in out_shape[2:]), i, 0)
+        ),
         out_shape=jax.ShapeDtypeStruct(out_shape, F32),
         scratch_shapes=[pltpu.VMEM((GROUP, DEPTH, count), F32), *scratch],
         cost_estimate=pl.CostEstimate(
@@ -155,7 +295,7 @@
     )(feat, points, other, length[:, None], height[:, None])
 
 
-def middle(scale, cell_index, expr_table, latent, mixing, noise_prec):
+def middle(scale, chunks, cell_index, expr_table, latent, mixing, noise_prec):
     rows = cell_index.shape[0]
     table, genes = expr_table.shape
     lats = latent.shape[0]
@@ -172,12 +312,13 @@
         ],
         out_specs=[
             pl.BlockSpec((lats, tile), lambda i: (0, i)),
-            pl.BlockSpec((lats, rows), lambda i: (0, 0)),
+            pl.BlockSpec(chunks, lambda i: (0, 0, 0, 0)),
         ],
         out_shape=[
             jax.ShapeDtypeStruct((lats, genes), F32),
-            jax.ShapeDtypeStruct((lats, rows), F32),
-        ],
+            jax.ShapeDtypeStruct(chunks, F32),
+        ],
+        scratch_shapes=[pltpu.VMEM((lats, rows), F32)],
         compiler_params=pltpu.CompilerParams(vmem_limit_bytes=40 * 2**20),
     )(cell_index[:, None], expr_table, latent, mixing, noise_prec[None, :])
 
@@ -208,22 +349,51 @@
     rows = feat.shape[0]
     lats, count = ind_weights.shape
     local_latent = products(
-        forward_body, (lats, rows), [pltpu.VMEM((GROUP, rows, 128), F32)], feat, inducing, ind_weights, lengthscale, variance
-    )
-    swapped = lax.all_to_all(local_latent, "lat", split_axis=1, concat_axis=0, tiled=True)
-    summed = lax.psum_scatter(swapped, "sub", scatter_dimension=1, tiled=True).astype(BF16)
-    latent = lax.all_gather(summed, "gene", axis=1, tiled=True)
+        forward_body, (block_count, lats, per_block), [pltpu.VMEM((GROUP, rows, 128), F32)], feat, inducing, ind_weights, lengthscale, variance
+    )
+    sizes = (gene_count, lat_count, sub_count)
+
+    def finish_latent(recv_ref, out_ref):
+        for gene in range(gene_count):
+            for lat in range(lat_count):
+                first = (gene * lat_count + lat) * sub_count
+                value = recv_ref[first]
+                for sub in range(1, sub_count):
+                    value = value + recv_ref[first + sub]
+                out_ref[lat * lats : (lat + 1) * lats, gene * per_block : (gene + 1) * per_block] = value
+
+    def finish_grad(recv_ref, out_ref):
+        for block in range(block_count):
+            value = recv_ref[block]
+            for gene in range(1, gene_count):
+                value = value + recv_ref[gene * block_count + block]
+            out_ref[:, block * per_block : (block + 1) * per_block] = value
+
+    latent = exchange(
+        sizes,
+        lambda peer: peer[1] * sub_count + peer[2],
+        finish_latent,
+        jax.ShapeDtypeStruct((lat_count * lats, bat_rows), F32),
+        0,
+        local_latent,
+    ).astype(BF16)
     grad_scale = -1.0 / math.sqrt(bat_rows * block_count)
-    mixing_term, cell_term = middle(grad_scale, cell_index, expr_table, latent, mixing, noise_prec)
+    chunks = (gene_count, lat_count, lats, per_block)
+    mixing_term, cell_term = middle(grad_scale, chunks, cell_index, expr_table, latent, mixing, noise_prec)
     grad_mixing = lax.psum(mixing_term, ("lat", "sub"))
-    shared = lax.psum_scatter(cell_term, "gene", scatter_dimension=1, tiled=True)
-    paired = lax.all_gather(shared, "sub", axis=1, tiled=True)
-    latent_grad = lax.all_to_all(paired, "lat", split_axis=0, concat_axis=1, tiled=True)
+    latent_grad = exchange(
+        sizes,
+        lambda peer: peer[0] * lat_count + peer[1],
+        finish_grad,
+        jax.ShapeDtypeStruct((lats, rows), F32),
+        1,
+        cell_term.reshape(gene_count * lat_count, lats, per_block),
+    )
     scratch = [pltpu.VMEM((GROUP, rows, 128), F32), pltpu.VMEM((GROUP, 8, count), F32)]
     partial_inducing = products(
         backward_body, (lats, count), scratch, feat, inducing, latent_grad, lengthscale, variance
     )
-    grad_inducing = lax.psum(partial_inducing, "gene")
+    grad_inducing = gene_sum(gene_count, 2, partial_inducing)
     return (grad_mixing, grad_inducing)
 
 

time: 199 us -> 151 us (0.76)
  waiting for transfers between devices: 70 us -> 0.04 us
  Pallas kernels: 64.5 us -> 115 us
  blocking collectives: 35.1 us -> 6.01 us
    pallas_call x0 -> x3, Pallas kernels: none -> 50.3 us  [the longest x1 26.4 us: gene_sum(): pl.pallas_call(functools.partial(gene_sum_body, genes), in_specs=[pl.Bloc...]
    psum x1 -> x0, waiting for transfers between devices: 41.7 us -> none  [on_device(): grad_inducing = lax.psum(partial_inducing, 'gene')]
    unnamed x6 -> x1, waiting for transfers between devices: 28.3 us -> 0.02 us
    all_gather x2 -> x0, blocking collectives: 15.4 us -> none  [the longest x1 13.4 us: on_device(): latent = lax.all_gather(summed, 'gene', axis=1, tiled=True)]
    all_to_all x2 -> x0, blocking collectives: 13.6 us -> none  [the longest x1 7.03 us: on_device(): lax.all_to_all(local_latent, 'lat', split_axis=1, concat_axis=0, tiled=True)]
    unnamed x20 -> x23, local copies, waits for them, and re-layouts: 11 us -> 9.65 us
  transfers between devices with their start and end apart: 4 -> 1, of which waited for: 3 -> 0; matrix products, arithmetic and copies ran while one was open for 0% -> 0% of each run, Pallas kernels for 15% -> 45%
where the time goes in v2:
time: 151 us; the launch traced here: 150 us
  Pallas kernels  115 us (76%)
  between operations  14.2 us (9%)
  local copies, waits for them, and re-layouts  12.2 us (8%)
  blocking collectives  6.01 us (4%)
  other arithmetic  1.75 us (1%)
    pallas_call x2, Pallas kernels, products(): pl.pallas_call(functools.partial(body, tile), grid=(lats // GROUP,), in_s...  56.7 us
    pallas_call x1, Pallas kernels, gene_sum(): pl.pallas_call(functools.partial(gene_sum_body, genes), in_specs=[pl.Bloc...  26.4 us
    pallas_call x2, Pallas kernels, exchange(): pl.pallas_call(functools.partial(exchange_body, sizes, chunk_of, finish),...  23.9 us
    unnamed x23, local copies, waits for them, and re-layouts  9.65 us
    pallas_call x1, Pallas kernels, middle(): pl.pallas_call(functools.partial(middle_body, scale), grid=(genes // tile...  8.28 us
    all_gather x1, blocking collectives, on_device(): kernel_xy = lax.all_gather(local_xy, ('lat', 'sub'), axis=1, tiled=True)  6.01 us
  transfers between devices with their start and end apart: 1, of which 0 were waited for; matrix products, arithmetic and copies ran while one was open for 0% of the time, Pallas kernels for 45%

profile of v2, /device:TPU:0, one launch (start us, length us, event | category | flops | bytes accessed | tf_op | source)
XLA Modules:
  0.0 149.5 jit_solution(13949871368242998171)
XLA Ops:
  7.2 0.0 all-reduce.2.cloned.1.call-start
  7.2 0.7 copy.45.length_ref
  8.0 0.7 copy.46.height_ref
  8.7 0.8 dynamic_slice.3
  9.4 0.1 iota_compare_fusion
  9.5 0.8 select_reduce_fusion
  10.3 6.0 %all-gather = f32[4,64,2]{1,2,0:T(2,128)S(1)} all-gather(f32[1,64,2]{1,2,0:T(2,128)S(1)} %bitcast.36), channel_id=1, replica_groups=mesh['group'=2,'gene'=4,'lat'=2,'sub'=2] {'lat','sub'}, dimensions={0}, use_global_device_ids=true | all-gather | bytes 2560 | tf_op jit(solution)/shard_map/all_gather | solution.py:347
  16.3 0.1 reshape.146
  16.5 0.1 stack.9
  16.6 0.1 copy.44.feat_ref
  16.7 1.2 copy-done.6
  18.0 1.0 copy-done.8
  19.0 28.5 %shard_map.104.send_ref = f32[4,32,64]{2,1,0:T(8,128)S(1)} custom-call(bf16[256,24]{1,0:T(8,128)(2,1)S(1)} %copy.44.feat_ref, f32[2,32,4096]{2,1,0:T(8,128)S(1)} %copy-done.6, f32[32,4096]{1,0:T(8,128)S(1)} %copy-done.8, f32[32,1]{1,0:T(8,128)S(1)} %copy.45.length_ref, f32[32,1]{1,0:T(8,128)S(1)} %copy.46.height_ref), custom_call_target="tpu_custom_call" | custom-call | flops 1610612736 | bytes 1572864 | tf_op jit(solution)/shard_map/pallas_call | solution.py:276
  47.5 0.6 copy-done.3
  48.1 11.7 %shard_map.105 = f32[64,256]{1,0:T(8,128)} custom-call(f32[4,32,64]{2,1,0:T(8,128)} %copy-done.3), custom_call_target="tpu_custom_call" | custom-call | tf_op jit(solution)/shard_map/pallas_call | solution.py:187
  59.9 0.8 convert_element_type.4.latent_ref
  60.7 0.0 copy-done.9
  60.7 0.1 copy.47.index_ref
  60.8 0.0 copy-done.1
  60.9 0.0 copy-done.5
  60.9 0.0 copy-start
  60.9 2.2 %copy-done = bf16[512,4096]{1,0:T(8,128)(2,1)S(1)} copy-done((bf16[512,4096]{1,0:T(8,128)(2,1)S(1)}, bf16[512,4096]{1,0:T(8,128)(2,1)}, u32[]{:S(2)}) %copy-start) | copy-done | bytes 4194328
  63.1 8.3 %shard_map.106 = (f32[64,4096]{1,0:T(8,128)}, f32[4,2,32,64]{3,2,1,0:T(8,128)S(1)}) custom-call(s32[256,1]{1,0:T(8,128)S(1)} %copy.47.index_ref, bf16[512,4096]{1,0:T(8,128)(2,1)S(1)} %copy-done, bf16[64,256]{1,0:T(8,128)(2,1)S(1)} %convert_element_type.4.latent_ref, bf16[64,4096]{1,0:T(8,128)(2,1)S(1)} %copy-done.1, f32[1,4096]{1,0:T(1,128)S(1)} %bitcast.34), custom_call_target="tpu_custom_call" | custom-call | tf_op jit(solution)/shard_map/pallas_call | solution.py:303
  71.3 0.7 copy-done.2
  72.0 0.0 all-reduce.2.cloned.1.call-update
  72.0 12.1 %shard_map.107.grad_ref = f32[32,256]{1,0:T(8,128)} custom-call(f32[8,32,64]{2,1,0:T(8,128)} %bitcast.33), custom_call_target="tpu_custom_call" | custom-call | tf_op jit(solution)/shard_map/pallas_call | solution.py:187
  84.2 0.7 copy-done.4
  84.9 28.2 %shard_map.108.x_ref = f32[32,4096]{1,0:T(8,128)S(1)} custom-call(bf16[256,24]{1,0:T(8,128)(2,1)S(1)} %copy.44.feat_ref, f32[2,32,4096]{2,1,0:T(8,128)S(1)} %copy-done.7, f32[32,256]{1,0:T(8,128)S(1)} %copy-done.4, f32[32,1]{1,0:T(8,128)S(1)} %copy.45.length_ref, f32[32,1]{1,0:T(8,128)S(1)} %copy.46.height_ref), custom_call_target="tpu_custom_call" | custom-call | flops 1610612736 | bytes 1572864 | tf_op jit(solution)/shard_map/pallas_call | solution.py:276
  113.2 26.4 %shard_map.109 = f32[32,4096]{1,0:T(8,128)S(1)} custom-call(f32[32,4096]{1,0:T(8,128)S(1)} %shard_map.108.x_ref), custom_call_target="tpu_custom_call" | custom-call | tf_op jit(solution)/shard_map/pallas_call | solution.py:251
  139.6 0.0 all-reduce.2.cloned.1.call-done
  139.6 2.3 %copy.53 = f32[64,4096]{1,0:T(8,128)} copy(f32[64,4096]{1,0:T(8,128)} %all-reduce.2.cloned.1.call-done) | data formatting | bytes 2097152
  141.9 0.8 copy.54
  (17 shorter events, 0.1 us)
Async XLA Ops:
  7.2 132.4 %all-reduce.2.cloned.1.call-start = ((), (), s32[]{:S(2)}) async-start(), calls=%async_computation | async-start | bytes 2097152 | tf_op jit(solution)/shard_map/psum | solution.py:383
  16.7 1.2 copy-start.6
  18.0 1.0 copy-start.8
  19.0 41.7 %copy-start.9 = (s32[256]{0:T(256)S(1)}, s32[256]{0:T(256)}, u32[]{:S(2)}) copy-start(s32[256]{0:T(256)} %param.9) | copy-start | bytes 3076
  19.0 41.9 %copy-start.1 = (bf16[64,4096]{1,0:T(8,128)(2,1)S(1)}, bf16[64,4096]{1,0:T(8,128)(2,1)}, u32[]{:S(2)}) copy-start(bf16[64,4096]{1,0:T(8,128)(2,1)} %mixing_ref.1) | copy-start | bytes 1572868
  19.0 41.9 %copy-start.5 = (f32[4096]{0:T(1024)S(1)}, f32[4096]{0:T(1024)}, u32[]{:S(2)}) copy-start(f32[4096]{0:T(1024)} %param.17) | copy-start | bytes 49156
  19.0 65.2 %copy-start.7 = (f32[2,32,4096]{2,1,0:T(8,128)S(1)}, f32[2,32,4096]{2,1,0:T(8,128)}, u32[]{:S(2)}) copy-start(f32[2,32,4096]{2,1,0:T(8,128)} %points_ref.3) | copy-start | bytes 3145732
  47.5 0.6 copy-start.3
  60.9 2.2 %copy-start = (bf16[512,4096]{1,0:T(8,128)(2,1)S(1)}, bf16[512,4096]{1,0:T(8,128)(2,1)}, u32[]{:S(2)}) copy-start(bf16[512,4096]{1,0:T(8,128)(2,1)} %expr_ref.1) | copy-start | bytes 12582916
  71.3 0.7 copy-start.2
  84.2 0.8 copy-start.4
Sparse Core Ops, SparseCore 0:
  72.1 39.3 all-reduce.1
